TPU v7x, 32 devices: a whole 2x2x4 slice. The times are simulated.
32 devices in a mesh: section: 4 (over x, core), mp: 8 (over z, y).
Axes of the slice: x: 2, y: 2, z: 4, core: 2. Of those that a mesh axis runs over, the one named last changes fastest.
Arguments:
- activations: bfloat16 [4, 64, 4096], P('section', 'mp'), may hold values from -24 to 24
- enc_weight: bfloat16 [4, 4096, 4096], P('section', None, 'mp'), may hold values from -0.046875 to 0.046875
- enc_bias: float32 [4096], P('mp'), may hold values from -4 to 4
- dec_weight: bfloat16 [4096, 4, 4096], P('mp', 'section'), may hold values from -2.1875 to 2.1875
- dec_bias: float32 [4, 4096], P('section'), may hold values from -3 to 3
Outputs:
- loss: float32 [], replicated
- grad_dec: bfloat16 [4096, 4, 4096], P('mp', 'section')
- grad_bias: float32 [4, 4096], P('section', 'mp')
All inputs are finite; a program needn't handle non-finite values.
Results may differ from a plain program's by a relative error of at most 0.009.
Values may be sent and summed in bfloat16 or wider, within the bound.
A program may use at most 64 MiB of HBM per device.

v0:
```python
import jax
import jax.numpy as jnp
from jax import lax
from jax.sharding import PartitionSpec as P

penalty_weight = 2.0


def local(activations, enc_weight, enc_bias, dec_weight, dec_bias):
    all_rows = lax.all_gather(activations[0], "mp", axis=0, tiled=True)
    token_count = all_rows.shape[0]
    partial_value = jnp.dot(all_rows, enc_weight[0], preferred_element_type=jnp.float32)
    w_dec = dec_weight[:, 0, :]
    layer_norm = jnp.sqrt(jnp.sum(jnp.square(w_dec.astype(jnp.float32)), axis=1) + 1e-06)
    pre_sum, norm_total = (
        lax.psum(partial_value.astype(jnp.bfloat16), "section").astype(jnp.float32),
        lax.psum(layer_norm.astype(jnp.bfloat16), "section").astype(jnp.float32),
    )
    latents = jnp.maximum(pre_sum + enc_bias[None, :], 0.0).astype(jnp.bfloat16)
    latent_float = latents.astype(jnp.float32)
    latent_sum = jnp.sum(latent_float, axis=0)
    penalty_part = penalty_weight / token_count * jnp.sum(latent_float * norm_total[None, :])
    penalty_part = jnp.where(lax.axis_index("section") == 0, penalty_part, 0.0)
    coef = penalty_weight * latent_sum / token_count / layer_norm
    col_width = w_dec.shape[1] // lax.axis_size("mp")
    first_col = lax.axis_index("mp") * col_width
    recon_t = lax.psum_scatter(
        lax.dot_general(
            w_dec, latents, (((0,), (1,)), ((), ())), preferred_element_type=jnp.float32
        ),
        "mp",
        scatter_dimension=0,
        tiled=True,
    )
    bias_cols = lax.dynamic_slice_in_dim(dec_bias[0], first_col, col_width, 0)
    x_cols = lax.dynamic_slice_in_dim(all_rows, first_col, col_width, 1)
    error_cols = recon_t + bias_cols[:, None] - x_cols.T.astype(jnp.float32)
    square_sum = jnp.sum(error_cols * error_cols)
    scaled = 2.0 * error_cols / token_count
    grad_rec_t = scaled.astype(jnp.bfloat16)
    grad_bias = jnp.sum(scaled, axis=1)[None, :]
    grad_sum = lax.dot_general(
        latents,
        lax.all_gather(grad_rec_t, "mp", axis=0, tiled=True),
        (((0,), (1,)), ((), ())),
        preferred_element_type=jnp.float32,
    )
    grad_dec = (grad_sum + coef[:, None] * w_dec.astype(jnp.float32)).astype(jnp.bfloat16)[
        :, None, :
    ]
    loss = lax.psum(square_sum / token_count + penalty_part, ("section", "mp"))
    return (loss, grad_dec, grad_bias)


def solution(mesh):
    in_specs = (
        P("section", "mp", None),
        P("section", None, "mp"),
        P("mp"),
        P("mp", "section", None),
        P("section", None),
    )
    out_specs = (P(), P("mp", "section", None), P("section", "mp"))
    return jax.shard_map(local, mesh=mesh, in_specs=in_specs, out_specs=out_specs, check_vma=False)
```

profile of v0, /device:TPU:0, one launch (start us, length us, event | category | flops | bytes accessed | tf_op | source)
XLA Modules:
  0.0 231.0 jit_solution(3103381486748929811)
XLA Ops:
  7.2 0.0 copy-start
  7.2 0.0 copy-start.2
  7.2 0.0 all-reduce.2.cloned.1.call-start
  7.2 33.2 %all-gather = bf16[1,64,4096]{2,1,0:T(8,128)(2,1)S(1)} all-gather(bf16[1,8,4096]{2,1,0:T(8,128)(2,1)} %param.5), channel_id=2, replica_groups=mesh['section'=4,'mp'=8] {'mp'}, dimensions={1}, use_global_device_ids=true | all-gather | bytes 589824 | tf_op jit(solution)/shard_map/all_gather | solution.py:10
  40.5 3.7 %fusion.7 = bf16[64,512]{1,0:T(8,128)(2,1)} fusion(bf16[1,4096,512]{2,1,0:T(8,128)(2,1)} %param.6, bf16[1,64,4096]{2,1,0:T(8,128)(2,1)S(1)} %all-gather), kind=kOutput, calls=%fused_computation.10 | convolution fusion | flops 268468224 | bytes 4784128 | tf_op jit(solution)/shard_map/dot_general | solution.py:12
  44.1 0.0 all-reduce.2.cloned.1.call-update
  44.2 0.0 reduce-scatter.2.cloned.1.call-start
  44.2 32.7 %all-reduce.2.cloned.1.call-done = bf16[64,512]{1,0:T(8,128)(2,1)} async-done(((bf16[64,512]{1,0:T(8,128)(2,1)}), bf16[64,512]{1,0:T(8,128)(2,1)}) %all-reduce.2.cloned.1.call-update) | async-done | bytes 65552 | tf_op jit(solution)/shard_map/psum | solution.py:16
  76.9 0.0 copy-done.2
  76.9 0.0 copy-start.1
  76.9 4.1 %convolution_bitcast_fusion = f32[4096,64]{0,1:T(8,128)} fusion(bf16[512,1,4096]{2,0,1:T(8,128)(2,1)} %param.8, bf16[64,512]{1,0:T(8,128)(2,1)} %all-reduce.2.cloned.1.call-done, f32[512]{0:T(512)S(1)} %copy-done.2), kind=kOutput, calls=%fused_computation.6 | convolution fusion | flops 268566528 | bytes 5310464 | tf_op jit(solution)/shard_map/dot_general | solution.py:28
  81.0 0.0 reduce-scatter.2.cloned.1.call-update
  81.1 3.1 %fusion = f32[512]{0:T(512)S(1)} fusion(bf16[512,1,4096]{2,0,1:T(8,128)(2,1)} %param.8), kind=kLoop, calls=%fused_computation.2 | loop fusion | flops 6290944 | bytes 4196352 | tf_op jit(solution)/shard_map/reduce_sum | solution.py:14
  84.1 5.8 %psum.22 = bf16[512]{0:T(512)(128)(2,1)S(1)} all-reduce(bf16[512]{0:T(512)(128)(2,1)S(1)} %sqrt_convert_fusion), channel_id=1, replica_groups=mesh['section'=4,'mp'=8] {'section'}, use_global_device_ids=true, to_apply=%region_4.0 | all-reduce | flops 512 | bytes 2048 | tf_op jit(solution)/shard_map/psum | solution.py:17
  89.9 0.0 copy-done
  89.9 0.0 copy-done.1
  89.9 0.6 convert_reduce_fusion
  91.2 54.2 %reduce-scatter.2.cloned.1.call-done = f32[512,64]{0,1:T(8,128)} async-done(((f32[4096,64]{0,1:T(8,128)}), f32[512,64]{0,1:T(8,128)}) %reduce-scatter.2.cloned.1.call-update) | async-done | bytes 131088 | tf_op jit(solution)/shard_map/reduce_scatter | solution.py:27
  145.5 1.5 multiply_reduce_fusion.1
  147.7 39.8 %psum.23 = f32[]{:T(128)} all-reduce(f32[]{:T(128)S(6)} %add.54), channel_id=1, replica_groups=mesh['section'=4,'mp'=8] {'section','mp'}, use_global_device_ids=true, to_apply=%region_6.7 | all-reduce | flops 1 | bytes 8 | tf_op jit(solution)/shard_map/psum | solution.py:51
  187.5 31.2 %all_gather.7 = bf16[4096,64]{0,1:T(8,128)(2,1)S(1)} all-gather(bf16[512,64]{0,1:T(8,128)(2,1)S(1)} %get-tuple-element.7), channel_id=1, replica_groups=mesh['section'=4,'mp'=8] {'mp'}, dimensions={0}, use_global_device_ids=true | all-gather | bytes 589824 | tf_op jit(solution)/shard_map/all_gather | solution.py:44
  218.7 5.5 %fusion.3 = bf16[512,1,4096]{2,0,1:T(8,128)(2,1)} fusion(bf16[4096,64]{0,1:T(8,128)(2,1)S(1)} %all_gather.7, bf16[512,1,4096]{2,0,1:T(8,128)(2,1)} %param.8, f32[512]{0:T(512)S(1)} %rsqrt_multiply_fusion, bf16[64,512]{1,0:T(8,128)(2,1)S(1)} %copy-done.1, f32[512]{0:T(512)S(1)} %copy-done.2), kind=kOutput, calls=%fused_computation.5 | convolution fusion | flops 276955136 | bytes 8982528 | tf_op jit(solution)/shard_map/dot_general | solution.py:42
  (4 shorter events, 0.0 us)
Async XLA Ops:
  7.2 82.8 %copy-start = (f32[1,4096]{1,0:T(1,128)S(1)}, f32[1,4096]{1,0:T(1,128)}, u32[]{:S(2)}) copy-start(f32[1,4096]{1,0:T(1,128)} %param.9) | copy-start | bytes 49156
  7.2 69.8 %copy-start.2 = (f32[512]{0:T(512)S(1)}, f32[512]{0:T(512)}, u32[]{:S(2)}) copy-start(f32[512]{0:T(512)} %param.7) | copy-start | bytes 6148
  7.2 69.8 %all-reduce.2.cloned.1.call-start = ((), (), s32[]{:S(2)}) async-start(), calls=%async_computation.1 | async-start | bytes 131072 | tf_op jit(solution)/shard_map/psum | solution.py:16
  44.2 101.3 %reduce-scatter.2.cloned.1.call-start = ((), (), s32[]{:S(2)}) async-start(), calls=%async_computation.2 | async-start | bytes 1179648 | tf_op jit(solution)/shard_map/reduce_scatter | solution.py:27
  76.9 13.0 %copy-start.1 = (bf16[64,512]{1,0:T(8,128)(2,1)S(1)}, bf16[64,512]{1,0:T(8,128)(2,1)}, u32[]{:S(2)}) copy-start(bf16[64,512]{1,0:T(8,128)(2,1)} %all-reduce.2.cloned.1.call-done) | copy-start | bytes 196612
Sparse Core Ops, SparseCore 0:
  44.3 32.6 all-reduce.1
  81.2 64.2 reduce-scatter.1
where the time goes:
time: 231 us
  blocking collectives  110 us (48%)
  waiting for transfers between devices  87 us (38%)
  between operations  15.4 us (7%)
  matrix products  13.2 us (6%)
  other arithmetic  5.29 us (2%)
    reduce_scatter x1, waiting for transfers between devices, local(): lax.psum_scatter(lax.dot_general(w_dec, latents, (((0,), (1,)), ((), ()))...  54.2 us
    psum x1, blocking collectives, local(): loss = lax.psum(square_sum / token_count + penalty_part, ('section', 'mp'))  39.8 us
    all_gather x1, blocking collectives, local(): all_rows = lax.all_gather(activations[0], 'mp', axis=0, tiled=True)  33.2 us
    psum x1, waiting for transfers between devices, local(): lax.psum(partial_value.astype(jnp.bfloat16), 'section').astype(jnp.float32)  32.7 us
    all_gather x1, blocking collectives, local(): lax.all_gather(grad_rec_t, 'mp', axis=0, tiled=True)  31.2 us
    psum x1, blocking collectives, local(): lax.psum(layer_norm.astype(jnp.bfloat16), 'section').astype(jnp.float32)  5.77 us
    dot_general x1, matrix products, local(): lax.dot_general(latents, lax.all_gather(grad_rec_t, 'mp', axis=0, tiled=T...  5.49 us
  transfers between devices with their start and end apart: 2, of which 2 were waited for; matrix products, arithmetic and copies ran while one was open for 2% of the time, Pallas kernels for 0%

commit v1 on v0

--- a/solution.py
+++ b/solution.py
@@ -48,7 +48,9 @@
     grad_dec = (grad_sum + coef[:, None] * w_dec.astype(jnp.float32)).astype(jnp.bfloat16)[
         :, None, :
     ]
-    loss = lax.psum(square_sum / token_count + penalty_part, ("section", "mp"))
+    loss = jnp.sum(
+        lax.all_gather(square_sum / token_count + penalty_part, ("section", "mp")), axis=0
+    )
     return (loss, grad_dec, grad_bias)
 
 

time: 231 us -> 232 us (level)
    unnamed x0 -> x1, blocking collectives: none -> 39.8 us
    psum x1 -> x0, blocking collectives: 39.8 us -> none  [local(): loss = lax.psum(square_sum / token_count + penalty_part, ('section', 'mp'))]
where the time goes in v1:
time: 232 us
  blocking collectives  110 us (47%)
  waiting for transfers between devices  87 us (38%)
  between operations  15.4 us (7%)
  matrix products  13.2 us (6%)
  other arithmetic  5.89 us (3%)
    reduce_scatter x1, waiting for transfers between devices, local(): lax.psum_scatter(lax.dot_general(w_dec, latents, (((0,), (1,)), ((), ()))...  54.2 us
    unnamed x1, blocking collectives  39.8 us
    all_gather x1, blocking collectives, local(): all_rows = lax.all_gather(activations[0], 'mp', axis=0, tiled=True)  33.2 us
    psum x1, waiting for transfers between devices, local(): lax.psum(partial_value.astype(jnp.bfloat16), 'section').astype(jnp.float32)  32.7 us
    all_gather x1, blocking collectives, local(): lax.all_gather(grad_rec_t, 'mp', axis=0, tiled=True)  31.2 us
    psum x1, blocking collectives, local(): lax.psum(layer_norm.astype(jnp.bfloat16), 'section').astype(jnp.float32)  5.77 us
    dot_general x1, matrix products, local(): lax.dot_general(latents, lax.all_gather(grad_rec_t, 'mp', axis=0, tiled=T...  5.49 us
  transfers between devices with their start and end apart: 2, of which 2 were waited for; matrix products, arithmetic and copies ran while one was open for 2% of the time, Pallas kernels for 0%

profile of v1, /device:TPU:0, one launch (start us, length us, event | category | flops | bytes accessed | tf_op | source)
XLA Modules:
  0.0 231.8 jit_solution(10686152047950123566)
XLA Ops:
  7.2 0.0 copy-start
  7.2 0.0 copy-start.2
  7.2 0.0 all-reduce.3.cloned.1.call-start
  7.2 33.2 %all-gather = bf16[1,64,4096]{2,1,0:T(8,128)(2,1)S(1)} all-gather(bf16[1,8,4096]{2,1,0:T(8,128)(2,1)} %param.5), channel_id=2, replica_groups=mesh['section'=4,'mp'=8] {'mp'}, dimensions={1}, use_global_device_ids=true | all-gather | bytes 589824 | tf_op jit(solution)/shard_map/all_gather | solution.py:10
  40.5 3.7 %fusion.7 = bf16[64,512]{1,0:T(8,128)(2,1)} fusion(bf16[1,4096,512]{2,1,0:T(8,128)(2,1)} %param.6, bf16[1,64,4096]{2,1,0:T(8,128)(2,1)S(1)} %all-gather), kind=kOutput, calls=%fused_computation.10 | convolution fusion | flops 268468224 | bytes 4784128 | tf_op jit(solution)/shard_map/dot_general | solution.py:12
  44.1 0.0 all-reduce.3.cloned.1.call-update
  44.2 0.0 reduce-scatter.2.cloned.1.call-start
  44.2 32.7 %all-reduce.3.cloned.1.call-done = bf16[64,512]{1,0:T(8,128)(2,1)} async-done(((bf16[64,512]{1,0:T(8,128)(2,1)}), bf16[64,512]{1,0:T(8,128)(2,1)}) %all-reduce.3.cloned.1.call-update) | async-done | bytes 65552 | tf_op jit(solution)/shard_map/psum | solution.py:16
  76.9 0.0 copy-done.2
  76.9 0.0 copy-start.1
  76.9 4.1 %convolution_bitcast_fusion = f32[4096,64]{0,1:T(8,128)} fusion(bf16[512,1,4096]{2,0,1:T(8,128)(2,1)} %param.8, bf16[64,512]{1,0:T(8,128)(2,1)} %all-reduce.3.cloned.1.call-done, f32[512]{0:T(512)S(1)} %copy-done.2), kind=kOutput, calls=%fused_computation.6 | convolution fusion | flops 268566528 | bytes 5310464 | tf_op jit(solution)/shard_map/dot_general | solution.py:28
  81.0 0.0 reduce-scatter.2.cloned.1.call-update
  81.1 3.1 %fusion = f32[512]{0:T(512)S(1)} fusion(bf16[512,1,4096]{2,0,1:T(8,128)(2,1)} %param.8), kind=kLoop, calls=%fused_computation.2 | loop fusion | flops 6290944 | bytes 4196352 | tf_op jit(solution)/shard_map/reduce_sum | solution.py:14
  84.1 5.8 %psum.15 = bf16[512]{0:T(512)(128)(2,1)S(1)} all-reduce(bf16[512]{0:T(512)(128)(2,1)S(1)} %sqrt_convert_fusion), channel_id=1, replica_groups=mesh['section'=4,'mp'=8] {'section'}, use_global_device_ids=true, to_apply=%region_4.0 | all-reduce | flops 512 | bytes 2048 | tf_op jit(solution)/shard_map/psum | solution.py:17
  89.9 0.0 copy-done
  89.9 0.0 copy-done.1
  89.9 0.6 convert_reduce_fusion
  91.2 54.2 %reduce-scatter.2.cloned.1.call-done = f32[512,64]{0,1:T(8,128)} async-done(((f32[4096,64]{0,1:T(8,128)}), f32[512,64]{0,1:T(8,128)}) %reduce-scatter.2.cloned.1.call-update) | async-done | bytes 131088 | tf_op jit(solution)/shard_map/reduce_scatter | solution.py:27
  145.5 1.5 multiply_reduce_fusion.1
  147.7 0.1 dynamic-update-slice
  147.8 39.8 %all-reduce = f32[32]{0:T(128)S(1)} all-reduce(f32[32]{0:T(128)S(1)} %dynamic-update-slice), channel_id=1, replica_groups=mesh['section'=4,'mp'=8] {'section','mp'}, use_global_device_ids=true, to_apply=%add | all-reduce | flops 32 | bytes 256
  187.6 0.6 reduce_sum.57
  188.2 31.2 %all_gather.15 = bf16[4096,64]{0,1:T(8,128)(2,1)S(1)} all-gather(bf16[512,64]{0,1:T(8,128)(2,1)S(1)} %get-tuple-element.7), channel_id=1, replica_groups=mesh['section'=4,'mp'=8] {'mp'}, dimensions={0}, use_global_device_ids=true | all-gather | bytes 589824 | tf_op jit(solution)/shard_map/all_gather | solution.py:44
  219.4 5.5 %fusion.3 = bf16[512,1,4096]{2,0,1:T(8,128)(2,1)} fusion(bf16[4096,64]{0,1:T(8,128)(2,1)S(1)} %all_gather.15, bf16[512,1,4096]{2,0,1:T(8,128)(2,1)} %param.8, f32[512]{0:T(512)S(1)} %rsqrt_multiply_fusion, bf16[64,512]{1,0:T(8,128)(2,1)S(1)} %copy-done.1, f32[512]{0:T(512)S(1)} %copy-done.2), kind=kOutput, calls=%fused_computation.5 | convolution fusion | flops 276955136 | bytes 8982528 | tf_op jit(solution)/shard_map/dot_general | solution.py:42
  (5 shorter events, 0.0 us)
Async XLA Ops:
  7.2 82.8 %copy-start = (f32[1,4096]{1,0:T(1,128)S(1)}, f32[1,4096]{1,0:T(1,128)}, u32[]{:S(2)}) copy-start(f32[1,4096]{1,0:T(1,128)} %param.9) | copy-start | bytes 49156
  7.2 69.8 %copy-start.2 = (f32[512]{0:T(512)S(1)}, f32[512]{0:T(512)}, u32[]{:S(2)}) copy-start(f32[512]{0:T(512)} %param.7) | copy-start | bytes 6148
  7.2 69.8 %all-reduce.3.cloned.1.call-start = ((), (), s32[]{:S(2)}) async-start(), calls=%async_computation.1 | async-start | bytes 131072 | tf_op jit(solution)/shard_map/psum | solution.py:16
  44.2 101.3 %reduce-scatter.2.cloned.1.call-start = ((), (), s32[]{:S(2)}) async-start(), calls=%async_computation.2 | async-start | bytes 1179648 | tf_op jit(solution)/shard_map/reduce_scatter | solution.py:27
  76.9 13.0 %copy-start.1 = (bf16[64,512]{1,0:T(8,128)(2,1)S(1)}, bf16[64,512]{1,0:T(8,128)(2,1)}, u32[]{:S(2)}) copy-start(bf16[64,512]{1,0:T(8,128)(2,1)} %all-reduce.3.cloned.1.call-done) | copy-start | bytes 196612
Sparse Core Ops, SparseCore 0:
  44.3 32.6 all-reduce.2
  81.2 64.2 reduce-scatter.1
